TPU v7x, 256 devices: a whole 4x4x8 slice. The times are simulated.
256 devices in a mesh: col: 8 (over y, x_hi), row: 32 (over z, x_lo, core).
Axes of the slice: x: 4 (x_hi: 2, x_lo: 2; x = x_hi * 2 + x_lo), y: 4, z: 8, core: 2. Of those that a mesh axis runs over, the one named last changes fastest.
Arguments:
- weights: float32 [16384, 16384], P('row', 'col'), may hold values from -6 to 6
- factor_rows: bfloat16 [1024, 16384], P('row', 'col'), may hold values from -0.25 to 0.25
- diag_inverse: bfloat16 [8, 128, 128], replicated, as said below
- prune_tiles: int32 [128, 8], P('row'), may hold values 0 or 1
- pivot_order: int32 [8], replicated, may hold values from 0 to 127, as said below
Outputs:
- pruned_weights: float32 [16384, 16384], P('row', 'col')
Inputs may be any that keep to these rules, and one draw needn't show every extreme that they name: `pivot_order`: the 8 block numbers are distinct; block 0 and the last block are among them. `diag_inverse`: each block is upper triangular with positive diagonal.
All inputs are finite; a program needn't handle non-finite values. No bound on the sum of `prune_tiles` on one device may be relied on, other than what follows from the above.
Results may differ from a plain program's by a relative error of at most 0.0003.
Values may be sent and summed in bfloat16 or wider, within the bound.
A program may use at most 64 MiB of HBM per device.

v0:
```python
import jax
import jax.numpy as jnp
from jax import lax
from jax.sharding import PartitionSpec as P

BLOCK = 128
PIVOTS = 8


def broadcast(x, axis, root):
    mine = lax.axis_index(axis) == root
    return lax.psum(jnp.where(mine, x, jnp.zeros_like(x)), axis)


def share_errors(errors_local, owner_col):
    return broadcast(errors_local, "col", owner_col)


def shards(weights, factor_rows, diag_inverse, prune_tiles, pivot_order):
    cols_local = weights.shape[1]
    blocks_dev = cols_local // BLOCK
    col_index = lax.axis_index("col")
    factor_all = lax.all_gather(factor_rows, "row", axis=0, tiled=True)
    pruned_all = jnp.repeat(prune_tiles.astype(jnp.float32), BLOCK, axis=0)
    local_ids = col_index * blocks_dev + jnp.arange(blocks_dev, dtype=jnp.int32)
    current = weights
    finished = jnp.zeros((blocks_dev,), jnp.float32)
    for step in range(PIVOTS):
        block_id = pivot_order[step]
        owner_col = block_id // blocks_dev
        local_start = block_id % blocks_dev * BLOCK
        panel_now = lax.dynamic_slice_in_dim(current, local_start, BLOCK, 1)
        pruned = pruned_all[:, step : step + 1]
        errors_local = (
            jnp.dot(
                panel_now, diag_inverse[step].astype(jnp.float32), precision=lax.Precision.HIGHEST
            )
            * pruned
        )
        errors = share_errors(errors_local, owner_col)
        finished = jnp.maximum(finished, (local_ids == block_id).astype(jnp.float32))
        keep_cols = jnp.repeat(1.0 - finished, BLOCK)
        factor_step = factor_all[step * BLOCK : (step + 1) * BLOCK].astype(jnp.float32)
        update = jnp.dot(errors, factor_step, precision=lax.Precision.HIGHEST)
        current = current - update * keep_cols[None, :]
        old_slice = lax.dynamic_slice_in_dim(current, local_start, BLOCK, 1)
        new_slice = jnp.where(owner_col == col_index, panel_now * (1.0 - pruned), old_slice)
        current = lax.dynamic_update_slice_in_dim(current, new_slice, local_start, 1)
    return current


def solution(mesh):
    return jax.shard_map(
        shards,
        mesh=mesh,
        in_specs=(P("row", "col"), P("row", "col"), P(), P("row", None), P()),
        out_specs=P("row", "col"),
        check_vma=False,
    )
```

profile of v0, /device:TPU:2, one launch (start us, length us, event | category | flops | bytes accessed | tf_op | source)
XLA Modules:
  0.0 793.7 jit_solution(10899068732405653597)
XLA Ops:
  7.4 1.6 fusion.60
  11.6 0.7 convert_element_type.18
  12.2 0.1 broadcast_bitcast_fusion
  12.4 1.9 fusion.7
  14.3 0.0 all-gather.2.cloned.1.call-start
  14.4 0.5 all-gather.2.cloned.1.call-update
  14.9 0.0 all-reduce.11.cloned.1.call-start
  17.5 0.6 fusion.57
  18.2 4.9 fusion.56
  23.0 0.1 broadcast_bitcast_fusion.8
  23.1 83.1 %all-reduce.9.cloned.1.call-done = f32[512,128]{1,0:T(8,128)} async-done(((f32[512,128]{1,0:T(8,128)}), f32[512,128]{1,0:T(8,128)}) %all-reduce.9.cloned.1.call-update) | async-done | bytes 262160 | tf_op jit(solution)/shard_map/psum | solution.py:12
  106.2 4.5 multiply_subtract_fusion.7
  110.7 1.1 select_dynamic-update-slice_fusion.7
  111.8 2.0 copy-done.6
  113.8 1.0 fusion.6
  114.9 1.3 broadcast_subtract_fusion.13
  118.7 0.1 broadcast_bitcast_fusion.7
  118.7 83.3 %all-reduce.11.cloned.1.call-done = f32[512,128]{1,0:T(8,128)} async-done(((f32[512,128]{1,0:T(8,128)}), f32[512,128]{1,0:T(8,128)}) %all-reduce.11.cloned.1.call-update) | async-done | bytes 262160 | tf_op jit(solution)/shard_map/psum | solution.py:12
  202.1 4.5 multiply_subtract_fusion.6
  206.5 1.1 select_dynamic-update-slice_fusion.6
  207.7 2.0 copy-done
  209.7 1.0 fusion.5
  210.6 0.0 all-reduce.15.cloned.1.call-start
  210.7 1.9 broadcast_subtract_fusion.12
  214.8 0.1 broadcast_bitcast_fusion.6
  214.9 83.2 %all-reduce.13.cloned.1.call-done = f32[512,128]{1,0:T(8,128)} async-done(((f32[512,128]{1,0:T(8,128)}), f32[512,128]{1,0:T(8,128)}) %all-reduce.13.cloned.1.call-update) | async-done | bytes 262160 | tf_op jit(solution)/shard_map/psum | solution.py:12
  298.1 4.5 multiply_subtract_fusion.5
  302.6 1.1 select_dynamic-update-slice_fusion.5
  303.7 2.0 copy-done.1
  305.7 1.0 fusion.4
  306.6 0.0 all-reduce.17.cloned.1.call-start
  306.7 0.7 broadcast_subtract_fusion.10
  310.2 0.1 broadcast_bitcast_fusion.5
  310.3 83.8 %all-reduce.15.cloned.1.call-done = f32[512,128]{1,0:T(8,128)} async-done(((f32[512,128]{1,0:T(8,128)}), f32[512,128]{1,0:T(8,128)}) %all-reduce.15.cloned.1.call-update) | async-done | bytes 262160 | tf_op jit(solution)/shard_map/psum | solution.py:12
  394.1 4.5 multiply_subtract_fusion.4
  398.6 1.1 select_dynamic-update-slice_fusion.4
  399.7 2.0 copy-done.2
  401.7 1.0 fusion.3
  402.7 0.2 all-reduce.19.cloned.1.call-start
  405.2 0.1 broadcast_bitcast_fusion.4
  405.2 84.8 %all-reduce.17.cloned.1.call-done = f32[512,128]{1,0:T(8,128)} async-done(((f32[512,128]{1,0:T(8,128)}), f32[512,128]{1,0:T(8,128)}) %all-reduce.17.cloned.1.call-update) | async-done | bytes 262160 | tf_op jit(solution)/shard_map/psum | solution.py:12
  490.1 4.5 multiply_subtract_fusion.3
  494.6 1.1 select_dynamic-update-slice_fusion.3
  495.7 2.0 copy-done.3
  497.7 1.0 fusion.2
  498.6 0.0 all-reduce.21.cloned.1.call-start
  498.7 0.6 broadcast_subtract_fusion.8
  501.5 0.1 broadcast_bitcast_fusion.3
  501.6 84.5 %all-reduce.19.cloned.1.call-done = f32[512,128]{1,0:T(8,128)} async-done(((f32[512,128]{1,0:T(8,128)}), f32[512,128]{1,0:T(8,128)}) %all-reduce.19.cloned.1.call-update) | async-done | bytes 262160 | tf_op jit(solution)/shard_map/psum | solution.py:12
  586.1 4.5 multiply_subtract_fusion.2
  590.6 1.1 select_dynamic-update-slice_fusion.2
  591.7 2.0 copy-done.4
  593.7 1.0 fusion.1
  594.7 0.0 all-reduce.23.cloned.1.call-start
  597.2 0.1 broadcast_bitcast_fusion.2
  597.3 84.8 %all-reduce.21.cloned.1.call-done = f32[512,128]{1,0:T(8,128)} async-done(((f32[512,128]{1,0:T(8,128)}), f32[512,128]{1,0:T(8,128)}) %all-reduce.21.cloned.1.call-update) | async-done | bytes 262160 | tf_op jit(solution)/shard_map/psum | solution.py:12
  682.1 4.5 multiply_subtract_fusion.1
  686.6 1.1 select_dynamic-update-slice_fusion.1
  687.7 2.0 copy-done.5
  689.6 1.0 fusion
  690.6 0.1 broadcast_bitcast_fusion.1
  690.7 87.4 %all-reduce.23.cloned.1.call-done = f32[512,128]{1,0:T(8,128)} async-done(((f32[512,128]{1,0:T(8,128)}), f32[512,128]{1,0:T(8,128)}) %all-reduce.23.cloned.1.call-update) | async-done | bytes 262160 | tf_op jit(solution)/shard_map/psum | solution.py:12
  778.1 6.3 multiply_subtract_fusion
  784.4 1.9 select_dynamic-update-slice_fusion
  (21 shorter events, 0.2 us)
Async XLA Ops:
  7.4 98.9 %all-reduce.9.cloned.1.call-start = ((), (), s32[]{:S(2)}) async-start(), calls=%async_computation | async-start | bytes 524288 | tf_op jit(solution)/shard_map/psum | solution.py:12
  14.3 91.9 %all-gather.2.cloned.1.call-start = ((), (), s32[]{:S(2)}) async-start(), calls=%async_computation.1 | async-start | bytes 4325376 | tf_op jit(solution)/shard_map/all_gather | solution.py:23
  14.9 187.2 %all-reduce.11.cloned.1.call-start = ((), (), s32[]{:S(2)}) async-start(), calls=%async_computation.2 | async-start | bytes 524288 | tf_op jit(solution)/shard_map/psum | solution.py:12
  23.1 90.7 %copy-start.7 = (bf16[8,128,128]{2,1,0:T(8,128)(2,1)S(1)}, bf16[8,128,128]{2,1,0:T(8,128)(2,1)}, u32[]{:S(2)}) copy-start(bf16[8,128,128]{2,1,0:T(8,128)(2,1)} %param.7) | copy-start | bytes 786436
  111.8 2.0 copy-start.6
  114.8 183.3 %all-reduce.13.cloned.1.call-start = ((), (), s32[]{:S(2)}) async-start(), calls=%async_computation.3 | async-start | bytes 524288 | tf_op jit(solution)/shard_map/psum | solution.py:12
  207.6 2.0 copy-start
  210.6 183.4 %all-reduce.15.cloned.1.call-start = ((), (), s32[]{:S(2)}) async-start(), calls=%async_computation.4 | async-start | bytes 524288 | tf_op jit(solution)/shard_map/psum | solution.py:12
  303.6 2.0 copy-start.1
  306.6 183.4 %all-reduce.17.cloned.1.call-start = ((), (), s32[]{:S(2)}) async-start(), calls=%async_computation.5 | async-start | bytes 524288 | tf_op jit(solution)/shard_map/psum | solution.py:12
  399.7 2.0 copy-start.2
  402.7 183.4 %all-reduce.19.cloned.1.call-start = ((), (), s32[]{:S(2)}) async-start(), calls=%async_computation.6 | async-start | bytes 524288 | tf_op jit(solution)/shard_map/psum | solution.py:12
  495.6 2.0 copy-start.3
  498.6 183.4 %all-reduce.21.cloned.1.call-start = ((), (), s32[]{:S(2)}) async-start(), calls=%async_computation.7 | async-start | bytes 524288 | tf_op jit(solution)/shard_map/psum | solution.py:12
  591.7 2.0 copy-start.4
  594.7 183.4 %all-reduce.23.cloned.1.call-start = ((), (), s32[]{:S(2)}) async-start(), calls=%async_computation.8 | async-start | bytes 524288 | tf_op jit(solution)/shard_map/psum | solution.py:12
  687.7 2.0 copy-start.5
Sparse Core Ops, SparseCore 0:
  14.4 91.7 all-reduce.8
  114.9 87.1 all-reduce.10
  210.8 87.2 all-reduce.12
  306.8 87.2 all-reduce.14
  402.8 87.2 all-reduce.16
  498.8 87.2 all-reduce.18
  594.8 87.2 all-reduce.20
  690.7 87.2 all-reduce.22
Sparse Core Ops, SparseCore 1:
  16.8 69.3 all-gather.1
where the time goes:
time: 795 us; the launch traced here: 794 us
  waiting for transfers between devices  676 us (85%)
  matrix products  46.2 us (6%)
  between operations  35 us (4%)
  other arithmetic  20.1 us (3%)
  local copies, waits for them, and re-layouts  16.3 us (2%)
    psum x8, waiting for transfers between devices, broadcast(): return lax.psum(jnp.where(mine, x, jnp.zeros_like(x)), axis)  675 us
    dot_general x8, matrix products, shards(): update = jnp.dot(errors, factor_step, precision=lax.Precision.HIGHEST)  37.6 us
  transfers between devices with their start and end apart: 9, of which 8 were waited for; matrix products, arithmetic and copies ran while one was open for 1% of the time, Pallas kernels for 0%

commit v1 on v0

v1 whole, which is shorter than its diff:
```python
import jax
import jax.numpy as jnp
from jax import lax
from jax.experimental import pallas as pl
from jax.experimental.pallas import tpu as pltpu
from jax.sharding import PartitionSpec as P

BLOCK = 128
PIVOTS = 8
COLDEV = 8
ROWDEV = 32
Z = 8
CHUNK = 64
MESH = pl.DeviceIdType.MESH
ANY = pl.BlockSpec(memory_space=pl.ANY)
VM = pl.BlockSpec(memory_space=pltpu.VMEM)
SM = pl.BlockSpec(memory_space=pltpu.SMEM)


def prep_kernel(loc_ref, *refs):
    w_refs, f_refs = refs[:PIVOTS], refs[PIVOTS : 2 * PIVOTS]
    q_ref, s_ref, fp_ref = refs[2 * PIVOTS :]
    for k in range(PIVOTS):
        w = w_refs[k][...]
        top = jnp.maximum(jnp.max(jnp.abs(w), axis=0, keepdims=True), 1e-30)
        s_ref[0, k : k + 1, :] = top * (1.0 / 32767.0)
        q_ref[0, k] = jnp.round(w * (32767.0 / top)).astype(jnp.int32).astype(jnp.int16)

    @pl.when(pl.program_id(0) == 0)
    def _():
        for k in range(PIVOTS):
            fp_ref[k] = f_refs[k][...]


def prep(loc, weights, factor_rows):
    rows, frows = weights.shape[0], factor_rows.shape[0]
    chunks = rows // CHUNK

    def wspec(k):
        return pl.BlockSpec((CHUNK, BLOCK), lambda i, loc: (i, loc[k]))

    def fspec(k):
        return pl.BlockSpec((frows, BLOCK), lambda i, loc: (0, loc[k]))

    return pl.pallas_call(
        prep_kernel,
        grid_spec=pltpu.PrefetchScalarGridSpec(
            num_scalar_prefetch=1,
            grid=(chunks,),
            in_specs=[wspec(k) for k in range(PIVOTS)] + [fspec(k) for k in range(PIVOTS)],
            out_specs=[
                pl.BlockSpec((1, PIVOTS, CHUNK, BLOCK), lambda i, loc: (i, 0, 0, 0)),
                pl.BlockSpec((1, PIVOTS, BLOCK), lambda i, loc: (i, 0, 0)),
                pl.BlockSpec((PIVOTS, frows, BLOCK), lambda i, loc: (0, 0, 0)),
            ],
        ),
        out_shape=[
            jax.ShapeDtypeStruct((chunks, PIVOTS, CHUNK, BLOCK), jnp.int16),
            jax.ShapeDtypeStruct((chunks, PIVOTS, BLOCK), jnp.float32),
            jax.ShapeDtypeStruct((PIVOTS, frows, BLOCK), jnp.bfloat16),
        ],
        name="prep",
    )(loc, *[weights] * PIVOTS, *[factor_rows] * PIVOTS)


class Net:
    def __init__(self, send, recv, local):
        self.send, self.recv, self.local = send, recv, local
        self.sent, self.own_count = [], 0

    def remote(self, src, dst, device):
        i = len(self.sent)
        copy = pltpu.make_async_remote_copy(
            src_ref=src,
            dst_ref=dst,
            send_sem=self.send.at[i],
            recv_sem=self.recv.at[i],
            device_id=device,
            device_id_type=MESH,
        )
        copy.start()
        self.sent.append(copy)
        return copy

    def own(self, src, dst):
        copy = pltpu.make_async_copy(src, dst, self.local.at[self.own_count])
        self.own_count += 1
        copy.start()
        return copy

    def finish(self):
        for copy in self.sent:
            copy.wait_send()


class RowGather:
    def __init__(self, net, r, mine, out, half):
        core, xlo = lax.rem(r, 2), lax.rem(r // 2, 2)
        self.net, self.mine, self.out, self.half, self.r = net, mine, out, half, r
        self.sibling = r + 1 - 2 * core
        self.partner = r + 2 - 4 * xlo
        self.up, self.down = lax.rem(r + 4, ROWDEV), lax.rem(r + ROWDEV - 4, ROWDEV)
        self.flight, self.given = {}, []

    def origin(self, chain, step):
        base = self.r if chain == 0 else self.partner
        return lax.rem(base + 4 * step + ROWDEV, ROWDEV)

    def give(self, origin, src):
        self.given.append(self.net.remote(src, self.out.at[origin], {"row": self.sibling}))

    def launch(self, chain, step):
        a, b = self.origin(chain, -step), self.origin(chain, step)
        out, half = self.out, self.half
        if chain == 0 and step == 0:
            src_a = src_b = self.mine
        else:
            src_a, src_b = out.at[a], out.at[b]
        dst_a, dst_b = out.at[a], out.at[b]
        if step == 3:
            src_a, dst_a, src_b, dst_b = half(src_a, 0), half(dst_a, 0), half(src_b, 1), half(dst_b, 1)
        self.flight[chain] = (
            self.net.remote(src_a, dst_a, {"row": self.up}),
            self.net.remote(src_b, dst_b, {"row": self.down}),
        )

    def begin(self):
        self.first = self.net.remote(self.mine, self.out.at[self.r], {"row": self.partner})
        self.launch(0, 0)
        self.give(self.r, self.mine)

    def stage(self, i):
        if i == 0:
            self.first.wait_recv()
            self.launch(1, 0)
            self.give(self.partner, self.out.at[self.partner])
            return
        chain, step = (i - 1) % 2, (i - 1) // 2
        for copy in self.flight[chain]:
            copy.wait_recv()
        if step < 3:
            self.launch(chain, step + 1)
            for o in (self.origin(chain, -step - 1), self.origin(chain, step + 1)):
                self.give(o, self.out.at[o])
        else:
            o = self.origin(chain, 4)
            self.give(o, self.out.at[o])

    def finish(self):
        for copy in self.given:
            copy.wait_recv()


STAGES = 9


def comm_kernel(piv, q, s, fp, f, qo, so, fo, po, rq, rs, r1, selq, sels, sel1, send, recv, local):
    me = lax.axis_index("col")
    r = lax.axis_index("row")
    blocks_dev = f.shape[1] // BLOCK
    cols = [lax.rem(me + d, COLDEV) for d in range(1, COLDEV)]
    net = Net(send, recv, local)
    fg = RowGather(net, r, f, fo, lambda ref, h: ref.at[pl.ds(16 * h, 16), :])
    pg = RowGather(net, r, po.at[r], po, lambda ref, h: ref.at[pl.ds(4 * h, 4)])

    barrier = pltpu.get_barrier_semaphore()
    for c in cols:
        pl.semaphore_signal(barrier, inc=1, device_id={"col": c}, device_id_type=MESH)
    for n in (fg.sibling, fg.partner, fg.up, fg.down):
        pl.semaphore_signal(barrier, inc=1, device_id={"row": n}, device_id_type=MESH)
    pl.semaphore_wait(barrier, COLDEV - 1 + 4)

    def to_cols(src_of, dst):
        return [net.remote(src_of(c), dst, {"col": c}) for c in cols]

    fp1 = to_cols(lambda c: fp.at[c], r1.at[me])
    fp1_own = net.own(fp.at[me], r1.at[me])
    fg.begin()
    f_own = net.own(f, fo.at[r])

    fp1_own.wait()
    for copy in fp1:
        copy.wait_recv()
    sel1[...] = r1[piv[me] // blocks_dev]
    fp2 = to_cols(lambda c: sel1, po.at[r, me])
    fp2_own = net.own(sel1, po.at[r, me])

    w1 = to_cols(lambda c: q.at[c], rq.at[me]) + to_cols(lambda c: s.at[c], rs.at[me])
    w1_own = [net.own(q.at[me], rq.at[me]), net.own(s.at[me], rs.at[me])]

    fp2_own.wait()
    for copy in fp2:
        copy.wait_recv()
    pg.begin()
    fg.stage(0)
    pg.stage(0)
    for i in range(1, 5):
        pg.stage(i)
        fg.stage(i)

    for copy in w1_own:
        copy.wait()
    for copy in w1:
        copy.wait_recv()
    for k in range(PIVOTS):
        owner = piv[k] // blocks_dev
        selq[k] = rq[owner, k]
        sels[k : k + 1, :] = rs[owner, k : k + 1, :]
    w2 = to_cols(lambda c: selq, qo.at[me]) + to_cols(lambda c: sels, so.at[me])
    w2_own = [net.own(selq, qo.at[me]), net.own(sels, so.at[me])]

    for i in range(5, STAGES):
        pg.stage(i)
        fg.stage(i)
    for copy in w2_own:
        copy.wait()
    for copy in w2:
        copy.wait_recv()
    pg.finish()
    fg.finish()
    f_own.wait()
    net.finish()


def comm(pivot_order, q, s, fp, f):
    frows, width = f.shape
    copies = 6 * (COLDEV - 1) + 2 * (1 + 16 + 16)
    return pl.pallas_call(
        comm_kernel,
        in_specs=[SM, ANY, ANY, ANY, ANY],
        out_specs=[ANY] * 4,
        out_shape=[
            jax.ShapeDtypeStruct(q.shape, q.dtype),
            jax.ShapeDtypeStruct(s.shape, s.dtype),
            jax.ShapeDtypeStruct((ROWDEV, frows, width), f.dtype),
            jax.ShapeDtypeStruct((ROWDEV,) + fp.shape, fp.dtype),
        ],
        scratch_shapes=[
            pltpu.VMEM(q.shape, q.dtype),
            pltpu.VMEM(s.shape, s.dtype),
            pltpu.VMEM(fp.shape, fp.dtype),
            pltpu.VMEM(q.shape[1:], q.dtype),
            pltpu.VMEM(s.shape[1:], s.dtype),
            pltpu.VMEM(fp.shape[1:], fp.dtype),
            pltpu.SemaphoreType.DMA((copies,)),
            pltpu.SemaphoreType.DMA((copies,)),
            pltpu.SemaphoreType.DMA((8,)),
        ],
        compiler_params=pltpu.CompilerParams(collective_id=0, has_side_effects=True),
        name="comm",
    )(pivot_order, q, s, fp, f)


def split(x):
    hi = x.astype(jnp.bfloat16)
    return hi, (x - hi.astype(jnp.float32)).astype(jnp.bfloat16)


def dot(a, b):
    return jnp.dot(a, b, preferred_element_type=jnp.float32)


def update_kernel(steps, prune, w, f, q, s, fp, d, out, ehi, elo, pan):
    rows, width = w.shape
    tile = pl.program_id(0)

    def by_tile(values):
        at = lax.broadcasted_iota(jnp.int32, (rows, 1), 0) // BLOCK
        column = jnp.full((rows, 1), values[0], jnp.float32)
        for t in range(1, len(values)):
            column = jnp.where(at == t, values[t], column)
        return column

    @pl.when(tile == 0)
    def _():
        for k in range(PIVOTS):
            coded = q[:, k].astype(jnp.int32).astype(jnp.float32)
            panel = (coded * s[:, k : k + 1, :]).reshape(rows, BLOCK)
            if k > 0:
                depth = k * BLOCK
                factor = fp[: 4 * k, k].reshape(depth, BLOCK)
                panel = panel - (dot(ehi[:, :depth], factor) + dot(elo[:, :depth], factor))
            hi, lo = split(panel)
            errors = dot(hi, d[k]) + dot(lo, d[k])
            errors = errors * by_tile([prune[t, k].astype(jnp.float32) for t in range(rows // BLOCK)])
            hi, lo = split(errors)
            ehi[:, k * BLOCK : (k + 1) * BLOCK] = hi
            elo[:, k * BLOCK : (k + 1) * BLOCK] = lo

    depth = lax.broadcasted_iota(jnp.int32, (f.shape[0], BLOCK), 0) // BLOCK
    blocks = width // BLOCK
    parts = []
    for b in range(blocks):
        part = f[:, b * BLOCK : (b + 1) * BLOCK]
        parts.append(jnp.where(depth < steps[tile * blocks + b], part, jnp.zeros_like(part)))
    masked = jnp.concatenate(parts, axis=1)
    new = w[...] - (dot(ehi[...], masked) + dot(elo[...], masked))
    for b in range(blocks):
        step = steps[tile * blocks + b]
        for t in range(rows // BLOCK):
            pruned = prune[t, jnp.minimum(step, PIVOTS - 1)].astype(jnp.float32)
            keep = jnp.where(step < PIVOTS, 1.0 - pruned, 1.0)
            out[t * BLOCK : (t + 1) * BLOCK, b * BLOCK : (b + 1) * BLOCK] = (
                new[t * BLOCK : (t + 1) * BLOCK, b * BLOCK : (b + 1) * BLOCK] * keep
            )


def update(steps, prune, w, f, q, s, fp, d):
    rows, width = w.shape
    tile = 256
    whole = lambda a: pl.BlockSpec(a.shape, lambda i, *_: (0,) * a.ndim)
    return pl.pallas_call(
        update_kernel,
        grid_spec=pltpu.PrefetchScalarGridSpec(
            num_scalar_prefetch=2,
            grid=(width // tile,),
            in_specs=[
                pl.BlockSpec((rows, tile), lambda i, *_: (0, i)),
                pl.BlockSpec((f.shape[0], tile), lambda i, *_: (0, i)),
                whole(q),
                whole(s),
                whole(fp),
                whole(d),
            ],
            out_specs=pl.BlockSpec((rows, tile), lambda i, *_: (0, i)),
            scratch_shapes=[
                pltpu.VMEM((rows, f.shape[0]), jnp.bfloat16),
                pltpu.VMEM((rows, f.shape[0]), jnp.bfloat16),
                pltpu.VMEM((rows, BLOCK), jnp.float32),
            ],
        ),
        out_shape=jax.ShapeDtypeStruct(w.shape, w.dtype),
        compiler_params=pltpu.CompilerParams(vmem_limit_bytes=48 * 2**20),
        name="update",
    )(steps, prune, w, f, q, s, fp, d)


def shards(weights, factor_rows, diag_inverse, prune_tiles, pivot_order):
    blocks_dev = weights.shape[1] // BLOCK
    q, s, fp = prep(pivot_order % blocks_dev, weights, factor_rows)
    q, s, f, fp = comm(pivot_order, q, s, fp, factor_rows)
    f = f.reshape(-1, f.shape[-1])
    ids = lax.axis_index("col") * blocks_dev + jnp.arange(blocks_dev, dtype=jnp.int32)
    hit = ids[:, None] == pivot_order[None, :]
    steps = jnp.min(jnp.where(hit, jnp.arange(PIVOTS, dtype=jnp.int32)[None], PIVOTS), axis=1)
    return update(steps, prune_tiles, weights, f, q, s, fp, diag_inverse)


def solution(mesh):
    return jax.shard_map(
        shards,
        mesh=mesh,
        in_specs=(P("row", "col"), P("row", "col"), P(), P("row", None), P()),
        out_specs=P("row", "col"),
        check_vma=False,
    )
```

time: 795 us -> 87.8 us (0.11)
  the two profiles are of different devices: /device:TPU:2 before, /device:TPU:1 now
where the time goes in v1:
time: 87.8 us; the launch traced here: 86.8 us
  Pallas kernels  81.3 us (93%)
  local copies, waits for them, and re-layouts  3.57 us (4%)
  other arithmetic  1.92 us (2%)
    pallas_call x1, Pallas kernels, comm(): pl.pallas_call(comm_kernel, in_specs=[SM, ANY, ANY, ANY, ANY], out_specs=...  59.1 us
    pallas_call x1, Pallas kernels, update(): pl.pallas_call(update_kernel, grid_spec=pltpu.PrefetchScalarGridSpec(num_...  15.9 us
    pallas_call x1, Pallas kernels, prep(): pl.pallas_call(prep_kernel, grid_spec=pltpu.PrefetchScalarGridSpec(num_sc...  6.33 us
    unnamed x10, local copies, waits for them, and re-layouts  3.57 us

profile of v1, /device:TPU:1, one launch (start us, length us, event | category | flops | bytes accessed | tf_op | source)
XLA Modules:
  0.0 86.8 jit_solution(3517221651813405503)
XLA Ops:
  0.0 0.7 select_reduce_fusion.steps
  0.7 1.2 %and_select_fusion.loc_ref = s32[8]{0:T(128)} fusion(s32[8]{0:T(128)} %piv.1), kind=kLoop, calls=%fused_computation.3 | loop fusion | flops 88 | bytes 64 | tf_op jit(solution)/shard_map/jit(remainder)/select_n | solution.py:340
  1.9 0.0 copy-start.2
  1.9 0.0 copy-start.4
  1.9 6.3 %prep.1 = (s16[8,8,64,128]{3,2,1,0:T(8,128)(2,1)}, f32[8,8,128]{2,1,0:T(8,128)}, bf16[8,32,128]{2,1,0:T(8,128)(2,1)}) custom-call(s32[8]{0:T(128)} %and_select_fusion.loc_ref, f32[512,2048]{1,0:T(8,128)} %w.1, f32[512,2048]{1,0:T(8,128)} %w.1, f32[512,2048]{1,0:T(8,128)} %w.1, f32[512,2048]{1,0:T(8,128)} %w.1, f32[512,2048]{1,0:T(8,128)} %w.1, ...), custom_call_target="tpu_custom_call" | custom-call | tf_op jit(solution)/shard_map/prep/pallas_call | solution.py:45
  8.3 59.1 %comm.1 = (s16[8,8,64,128]{3,2,1,0:T(8,128)(2,1)}, f32[8,8,128]{2,1,0:T(8,128)}, bf16[32,32,2048]{2,1,0:T(8,128)(2,1)}, bf16[32,8,32,128]{3,2,1,0:T(8,128)(2,1)}) custom-call(s32[8]{0:T(128)} %piv.1, s16[8,8,64,128]{3,2,1,0:T(8,128)(2,1)} %get-tuple-element.12.q, f32[8,8,128]{2,1,0:T(8,128)} %get-tuple-element.13.s, ...), custom_call_target="tpu_custom_call" | custom-call | tf_op jit(solution)/shard_map/comm/pallas_call | solution.py:228
  67.4 0.0 copy-done.2
  67.4 0.0 copy-done.4
  67.4 0.0 copy-start
  67.4 1.6 %copy-done = bf16[32,8,32,128]{3,2,1,0:T(8,128)(2,1)S(1)} copy-done((bf16[32,8,32,128]{3,2,1,0:T(8,128)(2,1)S(1)}, bf16[32,8,32,128]{3,2,1,0:T(8,128)(2,1)}, u32[]{:S(2)}) %copy-start) | copy-done | bytes 2097176
  69.0 0.0 copy-start.1
  69.0 1.2 %copy-done.1 = s16[8,8,64,128]{3,2,1,0:T(8,128)(2,1)S(1)} copy-done((s16[8,8,64,128]{3,2,1,0:T(8,128)(2,1)S(1)}, s16[8,8,64,128]{3,2,1,0:T(8,128)(2,1)}, u32[]{:S(2)}) %copy-start.1) | copy-done | bytes 1048600
  70.2 0.0 copy-start.3
  70.2 0.8 copy-done.3
  71.0 15.9 %update.1 = f32[512,2048]{1,0:T(8,128)} custom-call(s32[16]{0:T(128)S(1)} %select_reduce_fusion.steps, s32[4,8]{1,0:T(4,128)S(1)} %copy-done.4, f32[512,2048]{1,0:T(8,128)} %w.1, bf16[1024,2048]{1,0:T(8,128)(2,1)} %bitcast.1, s16[8,8,64,128]{3,2,1,0:T(8,128)(2,1)S(1)} %copy-done.1, f32[8,8,128]{2,1,0:T(8,128)S(1)} %copy-done.3, ...), custom_call_target="tpu_custom_call" | custom-call | tf_op jit(solution)/shard_map/update/pallas_call | solution.py:312
  (1 shorter events, 0.0 us)
Async XLA Ops:
  1.9 65.4 %copy-start.2 = (bf16[8,128,128]{2,1,0:T(8,128)(2,1)S(1)}, bf16[8,128,128]{2,1,0:T(8,128)(2,1)}, u32[]{:S(2)}) copy-start(bf16[8,128,128]{2,1,0:T(8,128)(2,1)} %d.1) | copy-start | bytes 786436
  1.9 65.5 %copy-start.4 = (s32[4,8]{1,0:T(4,128)S(1)}, s32[4,8]{1,0:T(4,128)}, u32[]{:S(2)}) copy-start(s32[4,8]{1,0:T(4,128)} %prune.1) | copy-start | bytes 388
  67.4 1.6 %copy-start = (bf16[32,8,32,128]{3,2,1,0:T(8,128)(2,1)S(1)}, bf16[32,8,32,128]{3,2,1,0:T(8,128)(2,1)}, u32[]{:S(2)}) copy-start(bf16[32,8,32,128]{3,2,1,0:T(8,128)(2,1)} %get-tuple-element.18.fp) | copy-start | bytes 6291460
  69.0 1.2 %copy-start.1 = (s16[8,8,64,128]{3,2,1,0:T(8,128)(2,1)S(1)}, s16[8,8,64,128]{3,2,1,0:T(8,128)(2,1)}, u32[]{:S(2)}) copy-start(s16[8,8,64,128]{3,2,1,0:T(8,128)(2,1)} %get-tuple-element.16.q) | copy-start | bytes 3145732
  70.2 0.8 copy-start.3

commit v2 on v0

v2 whole, which is shorter than its diff:
```python
import functools

import jax
import jax.numpy as jnp
from jax import lax
from jax.experimental import pallas as pl
from jax.experimental.pallas import tpu as pltpu
from jax.sharding import PartitionSpec as P

BLOCK = 128
PIVOTS = 8
COLDEV = 8
ROWDEV = 32
Z = 8
CHUNK = 64
VMEM = 62 * 2**20
MESH = pl.DeviceIdType.MESH
ANY = pl.BlockSpec(memory_space=pl.ANY)
VM = pl.BlockSpec(memory_space=pltpu.VMEM)
SM = pl.BlockSpec(memory_space=pltpu.SMEM)


def once(copy):
    return [(None, copy)]


def each(cases, act):
    for when, copy in cases:
        if when is None:
            act(copy)
        else:
            pl.when(when)(lambda copy=copy: act(copy))


class Net:
    def __init__(self, send, recv, local):
        self.send, self.recv, self.local = send, recv, local
        self.sent, self.own_count = [], 0

    def make(self, i, src, dst, device, land=None):
        return pltpu.make_async_remote_copy(
            src_ref=src,
            dst_ref=dst,
            send_sem=self.send.at[i],
            recv_sem=self.recv.at[i if land is None else land],
            device_id=device,
            device_id_type=MESH,
        )

    def remote(self, src, dst, device):
        copy = self.make(len(self.sent), src, dst, device)
        copy.start()
        self.sent.append(once(copy))
        return copy

    def shard(self, out, origin, cut, device, arriving, src=None):
        i = len(self.sent)

        def cases(o, src):
            made = []
            for when, view in cut(o):
                made.append((when, self.make(i, view(out.at[o] if src is None else src), view(out.at[o]), device)))
            return made

        sends = cases(origin, src)
        each(sends, lambda copy: copy.start())
        self.sent.append(sends)
        lands = cases(arriving, None)
        return lambda: each(lands, lambda copy: copy.wait_recv())

    def some(self, sends, lands, land=None):
        i = len(self.sent)
        cases = [(when, self.make(i, src, dst, device, land)) for when, src, dst, device in sends]
        each(cases, lambda copy: copy.start())
        self.sent.append(cases)
        return lambda: self.take(lands, i)

    def take(self, lands, i):
        cases = [(when, self.make(i, ref, ref, {"row": lax.axis_index("row")})) for when, ref in lands]
        each(cases, lambda copy: copy.wait_recv())

    def own(self, src, dst):
        copy = pltpu.make_async_copy(src, dst, self.local.at[self.own_count])
        self.own_count += 1
        copy.start()
        return copy

    def blocks(self, src, dst):
        sem = self.local.at[self.own_count]
        self.own_count += 1
        for b in range(dst.shape[0]):
            pltpu.make_async_copy(src.at[:, pl.ds(b * BLOCK, BLOCK)], dst.at[b], sem).start()
        return pltpu.make_async_copy(dst, dst, sem)

    def finish(self):
        for cases in self.sent:
            each(cases, lambda copy: copy.wait_send())


class Row:
    def __init__(self):
        r = lax.axis_index("row")
        core, xlo = lax.rem(r, 2), lax.rem(r // 2, 2)
        self.me, self.core, self.z = r, core, r // 4
        self.group = 2 * core + xlo
        self.sibling = r + 1 - 2 * core
        self.partner = r + 2 - 4 * xlo
        self.across = self.sibling + self.partner - r
        self.up, self.down = self.along(r, 1), self.along(r, -1)

    def along(self, base, steps):
        return lax.rem(base + 4 * steps + ROWDEV, ROWDEV)


def row_gather(net, row, out, cut, half, mine=None):
    given = []

    def give(origin, arriving, src=None):
        given.append(net.shard(out, origin, cut, {"row": row.sibling}, arriving, src))

    def launch(base, step, src=None):
        up, down = row.along(base, -step), row.along(base, step)
        part = [cut, cut] if step < 3 else [half(0), half(1)]
        return [
            net.shard(out, up, part[0], {"row": row.up}, row.along(base, -step - 1), src),
            net.shard(out, down, part[1], {"row": row.down}, row.along(base, step + 1), src),
        ]

    first = net.shard(out, row.me, cut, {"row": row.partner}, row.partner, mine)
    flight = [launch(row.me, 0, mine), None]
    give(row.me, row.sibling, mine)
    yield
    first()
    flight[1] = launch(row.partner, 0)
    give(row.partner, row.across)
    yield
    for step in range(4):
        for chain, base, other in ((0, row.me, row.sibling), (1, row.partner, row.across)):
            for landed in flight[chain]:
                landed()
            if step < 3:
                flight[chain] = launch(base, step + 1)
                give(row.along(base, -step - 1), row.along(other, -step - 1))
                give(row.along(base, step + 1), row.along(other, step + 1))
            else:
                give(row.along(base, 4), row.along(other, 4))
            yield
    for landed in given:
        landed()
    yield


def whole(origin):
    return [(None, lambda ref: ref)]


def rows_half(h):
    return lambda origin: [(None, lambda ref: ref.at[pl.ds(16 * h, 16), :])]


def split(x):
    hi = x.astype(jnp.bfloat16)
    return hi, (x - hi.astype(jnp.float32)).astype(jnp.bfloat16)


def dot(a, b):
    return jnp.dot(a, b, preferred_element_type=jnp.float32)


COPIES = 108
ORDER = "PFWPFFPFWFPWWPFPFWWRFRRFRRFRRR"


def comm_kernel(
    slots, piv, prune, w, f, d, fo, eo_hi, eo_lo,
    wv, fv, dv, fpv, r1, sel1, pv, q, s, rq, rs, selq, sels, qv, sv, ehi, elo, send, recv, local,
):
    me = lax.axis_index("col")
    row = Row()
    rows = w.shape[0]
    blocks_dev = f.shape[1] // BLOCK
    cols = [lax.rem(me + d, COLDEV) for d in (2, 6, 1, 7, 4, 3, 5)]
    planes = [1, -1, 2, -2, 3, -3, 4]
    net = Net(send, recv, local)

    load_f, load_w, load_d = net.blocks(f, fv), net.blocks(w, wv), net.own(d, dv)
    barrier = pltpu.get_barrier_semaphore()
    for c in cols:
        pl.semaphore_signal(barrier, inc=1, device_id={"col": c}, device_id_type=MESH)
    for n in [row.sibling, row.partner] + [row.along(row.me, p) for p in planes]:
        pl.semaphore_signal(barrier, inc=1, device_id={"row": n}, device_id_type=MESH)

    def to_cols(src_of, dst, peers=cols):
        return [net.remote(src_of(c), dst, {"col": c}) for c in peers]

    base = COPIES - PIVOTS

    def owners_of(k):
        return piv[k] // blocks_dev

    def place(k):
        return lax.rem(piv[k], blocks_dev)

    def factor():
        keep = net.own(f, fo.at[row.me])
        yield from row_gather(net, row, fo, whole, rows_half, f)
        keep.wait()
        yield

    def pivot_columns():
        load_f.wait()
        for k in range(1, PIVOTS):
            fpv[k] = fv[place(k)]
        pl.semaphore_wait(barrier, COLDEV - 1 + 9)
        hop = [net.some([(c > row.z, fpv.at[c], r1.at[me], {"col": c})], [(me > row.z, r1.at[me])]) for c in cols]
        yield
        for landed in hop:
            landed()

        @pl.when(me > row.z)
        def _():
            r1[me] = fpv[me]
            sel1[...] = r1[owners_of(me)]
            pv[me, row.group, row.z] = sel1[...]

        hop = []
        for p in planes:
            origin = row.along(row.me, -p) // 4
            hop.append(
                net.some(
                    [(me > row.z, sel1, pv.at[me, row.group, row.z], {"row": row.along(row.me, p)})],
                    [(me > origin, sel1)],
                )
            )
        yield
        for landed in hop:
            landed()
        for c in cols:
            sends = []
            for k in range(1, PIVOTS):
                above = pv.at[k, row.group, pl.ds(0, k)]
                sends.append((me == k, above, above, {"col": c}))
            net.some(sends, [], base + me)
        yield
        hop = []
        for k in range(1, PIVOTS):
            above = pv.at[k, row.group, pl.ds(0, k)]
            net.take([(me != k, above)], base + k)
            hop.append(net.some([(None, above, above, {"row": row.partner})], [(None, above)]))
        yield
        last = []
        for k, landed in zip(range(1, PIVOTS), hop):
            landed()
            above = pv.at[k, pl.ds(2 * row.core, 2), pl.ds(0, k)]
            last.append(net.some([(None, above, above, {"row": row.sibling})], [(None, above)]))
        yield
        for landed in last:
            landed()
        yield

    owners = [piv[k] // blocks_dev for k in range(PIVOTS)]
    ranks = [sum(((owners[i] == owners[k]).astype(jnp.int32) for i in range(k)), jnp.int32(0)) for k in range(PIVOTS)]

    def place_of_slot(i):
        start = jnp.int32(0)
        for k in range(PIVOTS):
            start = jnp.where((owners[k] == me) & (ranks[k] == i), place(k), start)
        return start

    def encode(chunk, qdst, sdst):
        rows_c = pl.ds(pl.multiple_of(chunk * CHUNK, CHUNK), CHUNK)
        for i in range(slots):
            block = wv[starts[i], rows_c]
            top = jnp.maximum(jnp.max(jnp.abs(block), axis=0, keepdims=True), 1e-30)
            sdst[i : i + 1, :] = top * (1.0 / 32767.0)
            qdst[i] = jnp.round(block * (32767.0 / top)).astype(jnp.int32).astype(jnp.int16)

    starts = [place_of_slot(i) for i in range(slots)]

    def panels():
        load_w.wait()
        hop = []
        for c in cols:
            encode(c, q.at[c], s.at[c])
            hop += to_cols(lambda c: s.at[c], rs.at[me], [c]) + to_cols(lambda c: q.at[c], rq.at[me], [c])
        encode(me, rq.at[me], rs.at[me])
        yield
        for copy in hop:
            copy.wait_recv()
        at_slot = lax.broadcasted_iota(jnp.int32, sels.shape, 0)
        for k in range(PIVOTS):
            slot = jnp.minimum(ranks[k], slots - 1)
            selq[k] = rq[owners[k], slot]
            picked = jnp.where(at_slot == slot, rs[owners[k]], 0.0)
            sels[k : k + 1, :] = jnp.sum(picked, axis=0, keepdims=True)
        beside = me + 1 - 2 * lax.rem(me, 2)
        ahead, behind = lax.rem(me + 2, COLDEV), lax.rem(me + 6, COLDEV)
        beside_ahead, beside_behind = lax.rem(beside + 2, COLDEV), lax.rem(beside + 6, COLDEV)
        across = net.remote(selq, qv.at[me], {"col": beside})
        first = [net.remote(selq, qv.at[me], {"col": c}) for c in (ahead, behind)]
        scales = to_cols(lambda c: sels, sv.at[me])
        keep = [net.own(selq, qv.at[me]), net.own(sels, sv.at[me])]
        yield
        across.wait_recv()
        second = [net.remote(qv.at[beside], qv.at[beside], {"col": c}) for c in (ahead, behind)]
        yield

        def pass_on(landed, from_behind, from_ahead):
            for copy in landed:
                copy.wait_recv()
            low, high = qv.at[from_behind, pl.ds(0, 4)], qv.at[from_ahead, pl.ds(4, 4)]
            return [net.remote(low, low, {"col": ahead}), net.remote(high, high, {"col": behind})]

        last = pass_on(first, behind, ahead)
        yield
        last += pass_on(second, beside_behind, beside_ahead)
        yield
        for copy in keep:
            copy.wait()
        for copy in last + scales:
            copy.wait_recv()
        yield

    def by_tile(values):
        at = lax.broadcasted_iota(jnp.int32, (rows, 1), 0) // BLOCK
        column = jnp.full((rows, 1), values[0], jnp.float32)
        for t in range(1, len(values)):
            column = jnp.where(at == t, values[t], column)
        return column

    def eliminate():
        load_d.wait()
        stores = []
        for k in range(PIVOTS):
            coded = qv[:, k].astype(jnp.int32).astype(jnp.float32)
            panel = (coded * sv[:, k : k + 1, :]).reshape(rows, BLOCK)
            if k > 0:
                depth = k * BLOCK
                block = jnp.concatenate([pv[k, g, j] for j in range(k) for g in (0, 2, 1, 3)], axis=0)
                panel = panel - (dot(ehi[:, :depth], block) + dot(elo[:, :depth], block))
            hi, lo = split(panel)
            errors = dot(hi, dv[k]) + dot(lo, dv[k])
            errors = errors * by_tile([prune[t, k].astype(jnp.float32) for t in range(rows // BLOCK)])
            hi, lo = split(errors)
            ehi[:, k * BLOCK : (k + 1) * BLOCK] = hi
            elo[:, k * BLOCK : (k + 1) * BLOCK] = lo
            yield
        stores = [net.own(ehi, eo_hi), net.own(elo, eo_lo)]
        yield
        for copy in stores:
            copy.wait()
        yield

    streams = {"P": pivot_columns, "F": factor, "W": panels, "R": eliminate}
    streams = {name: stream() for name, stream in streams.items()}
    for name in ORDER:
        next(streams[name], None)
    for stream in streams.values():
        for _ in stream:
            pass
    net.finish()


def comm(slots, pivot_order, prune, w, f, d):
    (rows, width), frows = w.shape, f.shape[0]
    chunks, depth = rows // CHUNK, PIVOTS * BLOCK
    q = pltpu.VMEM((chunks, PIVOTS, CHUNK, BLOCK), jnp.int16)
    s = pltpu.VMEM((chunks, PIVOTS, BLOCK), jnp.float32)
    sent_q = pltpu.VMEM((COLDEV, slots, CHUNK, BLOCK), jnp.int16)
    sent_s = pltpu.VMEM((COLDEV, PIVOTS, BLOCK), jnp.float32)
    columns = pltpu.VMEM((PIVOTS, frows, BLOCK), f.dtype)
    errors = pltpu.VMEM((rows, depth), jnp.bfloat16)
    return pl.pallas_call(
        functools.partial(comm_kernel, slots),
        in_specs=[SM, SM, ANY, ANY, ANY],
        out_specs=[ANY] * 3,
        out_shape=[
            jax.ShapeDtypeStruct((ROWDEV, frows, width), f.dtype),
            jax.ShapeDtypeStruct((rows, depth), jnp.bfloat16),
            jax.ShapeDtypeStruct((rows, depth), jnp.bfloat16),
        ],
        scratch_shapes=[
            pltpu.VMEM((width // BLOCK, rows, BLOCK), w.dtype),
            pltpu.VMEM((width // BLOCK, frows, BLOCK), f.dtype),
            pltpu.VMEM(d.shape, d.dtype),
            columns,
            columns,
            pltpu.VMEM((frows, BLOCK), f.dtype),
            pltpu.VMEM((PIVOTS, 4, Z, frows, BLOCK), f.dtype),
            sent_q,
            sent_s,
            sent_q,
            sent_s,
            pltpu.VMEM((PIVOTS, CHUNK, BLOCK), jnp.int16),
            pltpu.VMEM((PIVOTS, BLOCK), jnp.float32),
            q,
            s,
            errors,
            errors,
            pltpu.SemaphoreType.DMA((COPIES,)),
            pltpu.SemaphoreType.DMA((COPIES,)),
            pltpu.SemaphoreType.DMA((16,)),
        ],
        compiler_params=pltpu.CompilerParams(collective_id=0 if slots < PIVOTS else 1, has_side_effects=True, vmem_limit_bytes=VMEM),
        name="comm",
    )(pivot_order, prune, w, f, d)


def update_kernel(piv, prune, w, f, ehi, elo, out):
    rows, width = w.shape
    blocks = width // BLOCK
    total = pl.num_programs(0) * blocks
    first = lax.axis_index("col") * total + pl.program_id(0) * blocks
    steps = []
    for b in range(blocks):
        step = jnp.int32(PIVOTS)
        for k in range(PIVOTS):
            step = jnp.where(piv[k] == first + b, k, step)
        steps.append(step)

        @pl.loop(step, PIVOTS)
        def _(j, b=b):
            rows_j = pl.ds(pl.multiple_of(j * BLOCK, BLOCK), BLOCK)
            f[rows_j, b * BLOCK : (b + 1) * BLOCK] = jnp.zeros((BLOCK, BLOCK), f.dtype)

    new = w[...] - (dot(ehi[...], f[...]) + dot(elo[...], f[...]))
    for b, step in enumerate(steps):
        for t in range(rows // BLOCK):
            pruned = prune[t, jnp.minimum(step, PIVOTS - 1)].astype(jnp.float32)
            keep = jnp.where(step < PIVOTS, 1.0 - pruned, 1.0)
            here = slice(t * BLOCK, (t + 1) * BLOCK), slice(b * BLOCK, (b + 1) * BLOCK)
            out[here] = new[here] * keep


TILE = 512


def update(pivot_order, prune, w, f, ehi, elo):
    rows, width = w.shape
    resident = pl.BlockSpec(ehi.shape, lambda i, *_: (0, 0), pipeline_mode=pl.Buffered(1))
    return pl.pallas_call(
        update_kernel,
        grid_spec=pltpu.PrefetchScalarGridSpec(
            num_scalar_prefetch=2,
            grid=(width // TILE,),
            in_specs=[
                pl.BlockSpec((rows, TILE), lambda i, *_: (0, i)),
                pl.BlockSpec((f.shape[0], TILE), lambda i, *_: (0, i)),
                resident,
                resident,
            ],
            out_specs=pl.BlockSpec((rows, TILE), lambda i, *_: (0, i)),
        ),
        out_shape=jax.ShapeDtypeStruct(w.shape, w.dtype),
        compiler_params=pltpu.CompilerParams(vmem_limit_bytes=VMEM),
        name="update",
    )(pivot_order, prune, w, f, ehi, elo)


SLOTS = 4


def shards(weights, factor_rows, diag_inverse, prune_tiles, pivot_order):
    owners = pivot_order // (weights.shape[1] // BLOCK)
    most = jnp.max(jnp.sum((owners[:, None] == owners[None, :]).astype(jnp.int32), axis=1))
    f, ehi, elo = lax.cond(
        most <= SLOTS,
        functools.partial(comm, SLOTS),
        functools.partial(comm, PIVOTS),
        pivot_order,
        prune_tiles,
        weights,
        factor_rows,
        diag_inverse,
    )
    return update(pivot_order, prune_tiles, weights, f.reshape(-1, f.shape[-1]), ehi, elo)


def solution(mesh):
    return jax.shard_map(
        shards,
        mesh=mesh,
        in_specs=(P("row", "col"), P("row", "col"), P(), P("row", None), P()),
        out_specs=P("row", "col"),
        check_vma=False,
    )
```

time: 795 us -> 61.7 us (0.08)
  waiting for transfers between devices: 676 us -> 0 us
  Pallas kernels: 0 us -> 58.4 us
  matrix products: 46.2 us -> 0 us
  between operations: 35 us -> 0.66 us
  other arithmetic: 20.1 us -> 1.48 us
  local copies, waits for them, and re-layouts: 16.3 us -> 0 us
    psum x8 -> x0, waiting for transfers between devices: 675 us -> none  [broadcast(): return lax.psum(jnp.where(mine, x, jnp.zeros_like(x)), axis)]
    pallas_call x0 -> x2, Pallas kernels: none -> 58.4 us  [the longest x1 48.5 us: comm(): pl.pallas_call(functools.partial(comm_kernel, slots), in_specs=[SM, SM, A...]
    dot_general x16 -> x0, matrix products: 46.2 us -> none  [the longest x8 37.6 us: shards(): update = jnp.dot(errors, factor_step, precision=lax.Precision.HIGHEST)]
    unnamed x16 -> x0, local copies, waits for them, and re-layouts: 14 us -> none
    sub x7 -> x0, other arithmetic: 9.97 us -> none  [the longest x6 9.95 us: shards(): keep_cols = jnp.repeat(1.0 - finished, BLOCK)]
    dynamic_update_slice x8 -> x0, other arithmetic: 9.48 us -> none  [shards(): lax.dynamic_update_slice_in_dim(current, new_slice, local_start, 1)]
  transfers between devices with their start and end apart: 9 -> 0, of which waited for: 8 -> 0; matrix products, arithmetic and copies ran while one was open for 1% -> 0% of each run, Pallas kernels for 0% -> 0%
where the time goes in v2:
time: 61.7 us; the launch traced here: 60.8 us
  Pallas kernels  58.4 us (95%)
  other arithmetic  1.48 us (2%)
  between operations  0.66 us (1%)
    pallas_call x1, Pallas kernels, comm(): pl.pallas_call(functools.partial(comm_kernel, slots), in_specs=[SM, SM, A...  48.5 us
    pallas_call x1, Pallas kernels, update(): pl.pallas_call(update_kernel, grid_spec=pltpu.PrefetchScalarGridSpec(num_...  9.9 us

profile of v2, /device:TPU:2, one launch (start us, length us, event | category | flops | bytes accessed | tf_op | source)
XLA Modules:
  0.0 60.8 jit_solution(2310305782580089152)
XLA Ops:
  0.0 0.7 %and_select_fusion = s32[8]{0:T(128)S(1)} fusion(s32[8]{0:T(128)} %piv.1), kind=kLoop, calls=%fused_computation.1 | loop fusion | flops 120 | bytes 64 | tf_op jit(solution)/shard_map/jit(floor_divide)/jit(_where)/select_n | solution.py:464
  0.7 0.2 convert_reduce_fusion
  0.8 0.6 %reduce_max.9 = s32[]{:T(128)} reduce(s32[8]{0:T(128)S(1)} %convert_reduce_fusion, s32[]{:T(128)} %constant.19.clone.1), dimensions={0}, to_apply=%region_1.2 | reduce | flops 7 | bytes 40 | tf_op jit(solution)/shard_map/reduce_max | solution.py:465
  2.1 48.8 %conditional.1 = (bf16[512,1024]{1,0:T(8,128)(2,1)S(1)}, bf16[512,1024]{1,0:T(8,128)(2,1)}, bf16[1024,2048]{1,0:T(8,128)(2,1)}) conditional(s32[]{:T(128)} %convert_element_type.7, (s32[8]{0:T(128)}, s32[4,8]{1,0:T(4,128)}, f32[512,2048]{1,0:T(8,128)}, bf16[32,2048]{1,0:T(8,128)(2,1)}, bf16[8,128,128]{2,1,0:T(8,128)(2,1)}) %tuple.15, (s32[8]{0:T(128)}, ...), branch_computations={%region_2.3_spmd, %region_3.4_spmd} | conditional | bytes 24 | solution.py:466
  2.2 48.5 %comm.3 = (bf16[32,32,2048]{2,1,0:T(8,128)(2,1)}, bf16[512,1024]{1,0:T(8,128)(2,1)S(1)}, bf16[512,1024]{1,0:T(8,128)(2,1)}) custom-call(s32[8]{0:T(128)} %get-tuple-element.40.piv, s32[4,8]{1,0:T(4,128)} %get-tuple-element.41.prune, f32[512,2048]{1,0:T(8,128)} %get-tuple-element.42.w, bf16[32,2048]{1,0:T(8,128)(2,1)} %get-tuple-element.43.f, ...), custom_call_target="tpu_custom_call" | custom-call | tf_op jit(solution)/shard_map/cond/branch_1_fun/comm/pallas_call | solution.py:373
  50.9 9.9 %update.1 = f32[512,2048]{1,0:T(8,128)} custom-call(s32[8]{0:T(128)} %piv.1, s32[4,8]{1,0:T(4,128)} %prune.1, f32[512,2048]{1,0:T(8,128)} %w.1, bf16[1024,2048]{1,0:T(8,128)(2,1)} %get-tuple-element.51.f, bf16[512,1024]{1,0:T(8,128)(2,1)S(1)} %get-tuple-element.52.ehi, bf16[512,1024]{1,0:T(8,128)(2,1)} %get-tuple-element.53.elo), custom_call_target="tpu_custom_call" | custom-call | tf_op jit(solution)/shard_map/update/pallas_call | solution.py:441

commit v3 on v2

--- a/solution.py
+++ b/solution.py
@@ -13,7 +13,7 @@
 ROWDEV = 32
 Z = 8
 CHUNK = 64
-VMEM = 62 * 2**20
+VMEM = 58 * 2**20
 MESH = pl.DeviceIdType.MESH
 ANY = pl.BlockSpec(memory_space=pl.ANY)
 VM = pl.BlockSpec(memory_space=pltpu.VMEM)
@@ -112,11 +112,10 @@
         return lax.rem(base + 4 * steps + ROWDEV, ROWDEV)
 
 
-def row_gather(net, row, out, cut, half, mine=None):
-    given = []
-
-    def give(origin, arriving, src=None):
-        given.append(net.shard(out, origin, cut, {"row": row.sibling}, arriving, src))
+def row_gather(net, row, out, cut, half, mine, given):
+    def give(distance, origin, arriving, src=None):
+        landed = net.shard(out, origin, cut, {"row": row.sibling}, arriving, src)
+        given.setdefault(distance, []).append(landed)
 
     def launch(base, step, src=None):
         up, down = row.along(base, -step), row.along(base, step)
@@ -128,11 +127,11 @@
 
     first = net.shard(out, row.me, cut, {"row": row.partner}, row.partner, mine)
     flight = [launch(row.me, 0, mine), None]
-    give(row.me, row.sibling, mine)
+    give(0, row.me, row.sibling, mine)
     yield
     first()
     flight[1] = launch(row.partner, 0)
-    give(row.partner, row.across)
+    give(0, row.partner, row.across)
     yield
     for step in range(4):
         for chain, base, other in ((0, row.me, row.sibling), (1, row.partner, row.across)):
@@ -140,14 +139,11 @@
                 landed()
             if step < 3:
                 flight[chain] = launch(base, step + 1)
-                give(row.along(base, -step - 1), row.along(other, -step - 1))
-                give(row.along(base, step + 1), row.along(other, step + 1))
+                give(step + 1, row.along(base, -step - 1), row.along(other, -step - 1))
+                give(step + 1, row.along(base, step + 1), row.along(other, step + 1))
             else:
-                give(row.along(base, 4), row.along(other, 4))
+                give(4, row.along(base, 4), row.along(other, 4))
             yield
-    for landed in given:
-        landed()
-    yield
 
 
 def whole(origin):
@@ -168,12 +164,14 @@
 
 
 COPIES = 108
-ORDER = "PFWPFFPFWFPWWPFPFWWRFRRFRRFRRR"
+ORDER = "PFWPFPFWFPWFWPFPWFWFRRRRFRRRRFUFFFUU"
+BATCHES = ((0, -1, 1, -2, 2), (-3, 3, 4))
+SPAN = 1024
 
 
 def comm_kernel(
-    slots, piv, prune, w, f, d, fo, eo_hi, eo_lo,
-    wv, fv, dv, fpv, r1, sel1, pv, q, s, rq, rs, selq, sels, qv, sv, ehi, elo, send, recv, local,
+    slots, piv, prune, w, f, d, out,
+    wv, fv, dv, fpv, r1, sel1, pv, q, s, rq, rs, selq, sels, qv, sv, ev, fo, send, recv, local,
 ):
     me = lax.axis_index("col")
     row = Row()
@@ -201,11 +199,15 @@
     def place(k):
         return lax.rem(piv[k], blocks_dev)
 
+    given = {}
+
     def factor():
         keep = net.own(f, fo.at[row.me])
-        yield from row_gather(net, row, fo, whole, rows_half, f)
+        gather = row_gather(net, row, fo, whole, rows_half, f, given)
+        next(gather)
+        yield
         keep.wait()
-        yield
+        yield from gather
 
     def pivot_columns():
         load_f.wait()
@@ -330,28 +332,76 @@
 
     def eliminate():
         load_d.wait()
-        stores = []
+        panels = [
+            (qv[:, k].astype(jnp.int32).astype(jnp.float32) * sv[:, k : k + 1, :]).reshape(rows, BLOCK)
+            for k in range(PIVOTS)
+        ]
         for k in range(PIVOTS):
-            coded = qv[:, k].astype(jnp.int32).astype(jnp.float32)
-            panel = (coded * sv[:, k : k + 1, :]).reshape(rows, BLOCK)
-            if k > 0:
-                depth = k * BLOCK
-                block = jnp.concatenate([pv[k, g, j] for j in range(k) for g in (0, 2, 1, 3)], axis=0)
-                panel = panel - (dot(ehi[:, :depth], block) + dot(elo[:, :depth], block))
-            hi, lo = split(panel)
-            errors = dot(hi, dv[k]) + dot(lo, dv[k])
+            errors = dot(jnp.concatenate(split(panels[k]), axis=1), jnp.concatenate([dv[k], dv[k]], axis=0))
             errors = errors * by_tile([prune[t, k].astype(jnp.float32) for t in range(rows // BLOCK)])
             hi, lo = split(errors)
-            ehi[:, k * BLOCK : (k + 1) * BLOCK] = hi
-            elo[:, k * BLOCK : (k + 1) * BLOCK] = lo
+            ev[k, :, :BLOCK] = hi
+            ev[k, :, BLOCK:] = lo
+            both = jnp.concatenate([hi, lo], axis=1)
+            for n in range(k + 1, PIVOTS, 2):
+                ends = list(range(n, min(n + 2, PIVOTS)))
+                block = jnp.concatenate(
+                    [jnp.concatenate([pv[e, g, k] for g in (0, 2, 1, 3)], axis=0) for e in ends], axis=1
+                )
+                new = dot(both, jnp.concatenate([block, block], axis=0))
+                for i, e in enumerate(ends):
+                    panels[e] = panels[e] - new[:, i * BLOCK : (i + 1) * BLOCK]
             yield
-        stores = [net.own(ehi, eo_hi), net.own(elo, eo_lo)]
-        yield
-        for copy in stores:
-            copy.wait()
-        yield
-
-    streams = {"P": pivot_columns, "F": factor, "W": panels, "R": eliminate}
+
+    def step_of(block):
+        step = jnp.int32(PIVOTS)
+        for k in range(PIVOTS):
+            step = jnp.where((owners[k] == me) & (place(k) == block), k, step)
+        return step
+
+    def add(distances, last):
+        pivots = [lax.rem(row.z + p + Z, Z) for p in distances]
+        errors = jnp.concatenate([ev[j] for j in pivots], axis=1)
+        per = SPAN // BLOCK
+
+        @pl.loop(0, blocks_dev // per)
+        def _(i):
+            columns = pl.ds(pl.multiple_of(i * SPAN, SPAN), SPAN)
+            steps = [step_of(i * per + b) for b in range(per)]
+            parts = []
+            for j in pivots:
+                part = fo[pl.ds(4 * j, 4), :, columns].reshape(BLOCK, SPAN)
+                used = [
+                    jnp.full((BLOCK, BLOCK), jnp.where(j < step, 1.0, 0.0), jnp.float32).astype(f.dtype) for step in steps
+                ]
+                part = part * jnp.concatenate(used, axis=1)
+                parts += [part, part]
+            new = dot(errors, jnp.concatenate(parts, axis=0))
+            for b, step in enumerate(steps):
+                block = wv[i * per + b] - new[:, b * BLOCK : (b + 1) * BLOCK]
+                if last:
+                    kept = []
+                    for t in range(rows // BLOCK):
+                        pruned = prune[t, jnp.minimum(step, PIVOTS - 1)].astype(jnp.float32)
+                        kept.append(jnp.where(step < PIVOTS, 1.0 - pruned, 1.0))
+                    wv[i * per + b] = block * by_tile(kept)
+                else:
+                    wv[i * per + b] = block
+
+    def update():
+        for n, distances in enumerate(BATCHES):
+            for d in sorted({abs(p) for p in distances}):
+                for landed in given[d]:
+                    landed()
+            add(distances, n == len(BATCHES) - 1)
+            yield
+        stores = []
+        for b in range(blocks_dev):
+            pltpu.make_async_copy(wv.at[b], out.at[:, pl.ds(b * BLOCK, BLOCK)], local.at[15]).start()
+        pltpu.make_async_copy(wv, wv, local.at[15]).wait()
+        yield
+
+    streams = {"P": pivot_columns, "F": factor, "W": panels, "R": eliminate, "U": update}
     streams = {name: stream() for name, stream in streams.items()}
     for name in ORDER:
         next(streams[name], None)
@@ -369,16 +419,11 @@
     sent_q = pltpu.VMEM((COLDEV, slots, CHUNK, BLOCK), jnp.int16)
     sent_s = pltpu.VMEM((COLDEV, PIVOTS, BLOCK), jnp.float32)
     columns = pltpu.VMEM((PIVOTS, frows, BLOCK), f.dtype)
-    errors = pltpu.VMEM((rows, depth), jnp.bfloat16)
     return pl.pallas_call(
         functools.partial(comm_kernel, slots),
         in_specs=[SM, SM, ANY, ANY, ANY],
-        out_specs=[ANY] * 3,
-        out_shape=[
-            jax.ShapeDtypeStruct((ROWDEV, frows, width), f.dtype),
-            jax.ShapeDtypeStruct((rows, depth), jnp.bfloat16),
-            jax.ShapeDtypeStruct((rows, depth), jnp.bfloat16),
-        ],
+        out_specs=ANY,
+        out_shape=jax.ShapeDtypeStruct(w.shape, w.dtype),
         scratch_shapes=[
             pltpu.VMEM((width // BLOCK, rows, BLOCK), w.dtype),
             pltpu.VMEM((width // BLOCK, frows, BLOCK), f.dtype),
@@ -395,8 +440,8 @@
             pltpu.VMEM((PIVOTS, BLOCK), jnp.float32),
             q,
             s,
-            errors,
-            errors,
+            pltpu.VMEM((PIVOTS, rows, 2 * BLOCK), jnp.bfloat16),
+            pltpu.VMEM((ROWDEV, frows, width), f.dtype),
             pltpu.SemaphoreType.DMA((COPIES,)),
             pltpu.SemaphoreType.DMA((COPIES,)),
             pltpu.SemaphoreType.DMA((16,)),
@@ -406,65 +451,14 @@
     )(pivot_order, prune, w, f, d)
 
 
-def update_kernel(piv, prune, w, f, ehi, elo, out):
-    rows, width = w.shape
-    blocks = width // BLOCK
-    total = pl.num_programs(0) * blocks
-    first = lax.axis_index("col") * total + pl.program_id(0) * blocks
-    steps = []
-    for b in range(blocks):
-        step = jnp.int32(PIVOTS)
-        for k in range(PIVOTS):
-            step = jnp.where(piv[k] == first + b, k, step)
-        steps.append(step)
-
-        @pl.loop(step, PIVOTS)
-        def _(j, b=b):
-            rows_j = pl.ds(pl.multiple_of(j * BLOCK, BLOCK), BLOCK)
-            f[rows_j, b * BLOCK : (b + 1) * BLOCK] = jnp.zeros((BLOCK, BLOCK), f.dtype)
-
-    new = w[...] - (dot(ehi[...], f[...]) + dot(elo[...], f[...]))
-    for b, step in enumerate(steps):
-        for t in range(rows // BLOCK):
-            pruned = prune[t, jnp.minimum(step, PIVOTS - 1)].astype(jnp.float32)
-            keep = jnp.where(step < PIVOTS, 1.0 - pruned, 1.0)
-            here = slice(t * BLOCK, (t + 1) * BLOCK), slice(b * BLOCK, (b + 1) * BLOCK)
-            out[here] = new[here] * keep
-
-
-TILE = 512
-
-
-def update(pivot_order, prune, w, f, ehi, elo):
-    rows, width = w.shape
-    resident = pl.BlockSpec(ehi.shape, lambda i, *_: (0, 0), pipeline_mode=pl.Buffered(1))
-    return pl.pallas_call(
-        update_kernel,
-        grid_spec=pltpu.PrefetchScalarGridSpec(
-            num_scalar_prefetch=2,
-            grid=(width // TILE,),
-            in_specs=[
-                pl.BlockSpec((rows, TILE), lambda i, *_: (0, i)),
-                pl.BlockSpec((f.shape[0], TILE), lambda i, *_: (0, i)),
-                resident,
-                resident,
-            ],
-            out_specs=pl.BlockSpec((rows, TILE), lambda i, *_: (0, i)),
-        ),
-        out_shape=jax.ShapeDtypeStruct(w.shape, w.dtype),
-        compiler_params=pltpu.CompilerParams(vmem_limit_bytes=VMEM),
-        name="update",
-    )(pivot_order, prune, w, f, ehi, elo)
-
-
 SLOTS = 4
 
 
 def shards(weights, factor_rows, diag_inverse, prune_tiles, pivot_order):
     owners = pivot_order // (weights.shape[1] // BLOCK)
-    most = jnp.max(jnp.sum((owners[:, None] == owners[None, :]).astype(jnp.int32), axis=1))
-    f, ehi, elo = lax.cond(
-        most <= SLOTS,
+    pairs = jnp.sum((owners[:, None] == owners[None, :]).astype(jnp.int32))
+    return lax.cond(
+        pairs < (SLOTS + 1) ** 2 + PIVOTS - SLOTS - 1,
         functools.partial(comm, SLOTS),
         functools.partial(comm, PIVOTS),
         pivot_order,
@@ -473,7 +467,6 @@
         factor_rows,
         diag_inverse,
     )
-    return update(pivot_order, prune_tiles, weights, f.reshape(-1, f.shape[-1]), ehi, elo)
 
 
 def solution(mesh):

time: 61.7 us -> 54.8 us (0.89)
  Pallas kernels: 58.4 us -> 49.8 us
  local copies, waits for them, and re-layouts: 0 us -> 2.02 us
    pallas_call x1 -> x0, Pallas kernels: 9.9 us -> none  [update(): pl.pallas_call(update_kernel, grid_spec=pltpu.PrefetchScalarGridSpec(num_...]
    unnamed x0 -> x1, local copies, waits for them, and re-layouts: none -> 2.02 us
    pallas_call x1, Pallas kernels: 48.5 us -> 49.8 us  [comm(): pl.pallas_call(functools.partial(comm_kernel, slots), in_specs=[SM, SM, A...]
    reduce_max x1 -> x0, other arithmetic: 0.64 us -> none  [shards(): jnp.max(jnp.sum((owners[:, None] == owners[None, :]).astype(jnp.int32), a...]
where the time goes in v3:
time: 54.8 us; the launch traced here: 54.1 us
  Pallas kernels  49.8 us (91%)
  local copies, waits for them, and re-layouts  2.02 us (4%)
  other arithmetic  1.36 us (2%)
  between operations  0.66 us (1%)
    pallas_call x1, Pallas kernels, comm(): pl.pallas_call(functools.partial(comm_kernel, slots), in_specs=[SM, SM, A...  49.8 us
    unnamed x1, local copies, waits for them, and re-layouts  2.02 us

profile of v3, /device:TPU:2, one launch (start us, length us, event | category | flops | bytes accessed | tf_op | source)
XLA Modules:
  0.0 54.1 jit_solution(15716101353712482846)
XLA Ops:
  0.0 0.7 %and_select_fusion = s32[8]{0:T(128)S(1)} fusion(s32[8]{0:T(128)} %param.11), kind=kLoop, calls=%fused_computation.1 | loop fusion | flops 120 | bytes 64 | tf_op jit(solution)/shard_map/jit(floor_divide)/jit(_where)/select_n | solution.py:458
  0.7 0.7 %convert_reduce_fusion = s32[]{:T(128)} fusion(s32[8]{0:T(128)S(1)} %and_select_fusion), kind=kLoop, calls=%fused_computation | loop fusion | flops 191 | bytes 36 | tf_op jit(solution)/shard_map/reduce_sum | solution.py:459
  2.0 50.0 %conditional.1 = (f32[512,2048]{1,0:T(8,128)S(1)}) conditional(s32[]{:T(128)} %convert_element_type.7, (s32[8]{0:T(128)}, s32[4,8]{1,0:T(4,128)}, f32[512,2048]{1,0:T(8,128)}, bf16[32,2048]{1,0:T(8,128)(2,1)}, bf16[8,128,128]{2,1,0:T(8,128)(2,1)}) %tuple.11, (s32[8]{0:T(128)}, s32[4,8]{1,0:T(4,128)}, f32[512,2048]{1,0:T(8,128)}, ...), branch_computations={%region_1.2_spmd, %region_2.3_spmd} | conditional | bytes 8 | solution.py:460
  2.0 49.8 %comm.3 = f32[512,2048]{1,0:T(8,128)S(1)} custom-call(s32[8]{0:T(128)} %get-tuple-element.33.piv, s32[4,8]{1,0:T(4,128)} %get-tuple-element.34.prune, f32[512,2048]{1,0:T(8,128)} %get-tuple-element.35.w, bf16[32,2048]{1,0:T(8,128)(2,1)} %get-tuple-element.36.f, bf16[8,128,128]{2,1,0:T(8,128)(2,1)} %get-tuple-element.37.d), custom_call_target="tpu_custom_call" | custom-call | tf_op jit(solution)/shard_map/cond/branch_1_fun/comm/pallas_call | solution.py:422
  52.1 2.0 %copy.11 = f32[512,2048]{1,0:T(8,128)} copy(f32[512,2048]{1,0:T(8,128)S(1)} %get-tuple-element.38) | data formatting | bytes 8388608

commit v4 on v3

--- a/solution.py
+++ b/solution.py
@@ -35,49 +35,55 @@
 class Net:
     def __init__(self, send, recv, local):
         self.send, self.recv, self.local = send, recv, local
-        self.sent, self.own_count = [], 0
-
-    def make(self, i, src, dst, device, land=None):
+        self.sends = self.recvs = self.own_count = 0
+        self.sent = []
+
+    def new_send(self):
+        self.sends += 1
+        return self.sends - 1
+
+    def new_recv(self, count=1):
+        self.recvs += count
+        return self.recvs - count
+
+    def make(self, out, land, src, dst, device):
         return pltpu.make_async_remote_copy(
             src_ref=src,
             dst_ref=dst,
-            send_sem=self.send.at[i],
-            recv_sem=self.recv.at[i if land is None else land],
+            send_sem=self.send.at[out],
+            recv_sem=self.recv.at[land],
             device_id=device,
             device_id_type=MESH,
         )
 
+    def here(self, out, land, ref):
+        return self.make(out, land, ref, ref, {"row": lax.axis_index("row")})
+
+    def some(self, sends, lands, land=None, out=None):
+        land = self.new_recv() if land is None else land
+        group, out = out is not None, self.new_send() if out is None else out
+        cases = [(when, self.make(out, land, src, dst, device)) for when, src, dst, device in sends]
+        each(cases, lambda copy: copy.start())
+        if not group:
+            self.sent.append(cases)
+        return lambda: self.take(lands, land)
+
+    def take(self, lands, land):
+        each([(when, self.here(0, land, ref)) for when, ref in lands], lambda copy: copy.wait_recv())
+
     def remote(self, src, dst, device):
-        copy = self.make(len(self.sent), src, dst, device)
+        copy = self.make(self.new_send(), self.new_recv(), src, dst, device)
         copy.start()
         self.sent.append(once(copy))
         return copy
 
-    def shard(self, out, origin, cut, device, arriving, src=None):
-        i = len(self.sent)
-
-        def cases(o, src):
-            made = []
-            for when, view in cut(o):
-                made.append((when, self.make(i, view(out.at[o] if src is None else src), view(out.at[o]), device)))
-            return made
-
-        sends = cases(origin, src)
-        each(sends, lambda copy: copy.start())
-        self.sent.append(sends)
-        lands = cases(arriving, None)
-        return lambda: each(lands, lambda copy: copy.wait_recv())
-
-    def some(self, sends, lands, land=None):
-        i = len(self.sent)
-        cases = [(when, self.make(i, src, dst, device, land)) for when, src, dst, device in sends]
-        each(cases, lambda copy: copy.start())
-        self.sent.append(cases)
-        return lambda: self.take(lands, i)
-
-    def take(self, lands, i):
-        cases = [(when, self.make(i, ref, ref, {"row": lax.axis_index("row")})) for when, ref in lands]
-        each(cases, lambda copy: copy.wait_recv())
+    def group(self, copies, total):
+        out, land = self.new_send(), self.new_recv()
+        for src, dst, device in copies:
+            self.make(out, land, src, dst, device).start()
+        both = self.here(out, land, total)
+        self.sent.append(once(both))
+        return both
 
     def own(self, src, dst):
         copy = pltpu.make_async_copy(src, dst, self.local.at[self.own_count])
@@ -112,46 +118,50 @@
         return lax.rem(base + 4 * steps + ROWDEV, ROWDEV)
 
 
-def row_gather(net, row, out, cut, half, mine, given):
-    def give(distance, origin, arriving, src=None):
-        landed = net.shard(out, origin, cut, {"row": row.sibling}, arriving, src)
-        given.setdefault(distance, []).append(landed)
+def row_gather(net, row, out, mine, given):
+    group = net.new_send()
+    lands = [net.new_recv() for _ in range(5)]
+
+    def shard(origin, device, arriving, view=lambda ref: ref, src=None, land=None):
+        src = out.at[origin] if src is None else src
+        sends = [(None, view(src), view(out.at[origin]), {"row": device})]
+        return net.some(sends, [(None, view(out.at[arriving]))], land, group)
+
+    def give(distance, origin, src=None):
+        shard(origin, row.sibling, origin, src=src, land=lands[distance])
 
     def launch(base, step, src=None):
         up, down = row.along(base, -step), row.along(base, step)
-        part = [cut, cut] if step < 3 else [half(0), half(1)]
+        views = [lambda ref: ref] * 2 if step < 3 else [lambda ref, h=h: ref.at[pl.ds(16 * h, 16), :] for h in (0, 1)]
         return [
-            net.shard(out, up, part[0], {"row": row.up}, row.along(base, -step - 1), src),
-            net.shard(out, down, part[1], {"row": row.down}, row.along(base, step + 1), src),
+            shard(up, row.up, row.along(base, -step - 1), views[0], src),
+            shard(down, row.down, row.along(base, step + 1), views[1], src),
         ]
 
-    first = net.shard(out, row.me, cut, {"row": row.partner}, row.partner, mine)
+    net.sent.append(once(net.here(group, 0, out.at[pl.ds(0, 1 + 14 + 16)])))
+    for distance, land in enumerate(lands):
+        shards = out.at[pl.ds(0, 2 if distance in (0, 4) else 4)]
+        given[distance] = lambda shards=shards, land=land: net.take([(None, shards)], land)
+
+    first = shard(row.me, row.partner, row.partner, src=mine)
     flight = [launch(row.me, 0, mine), None]
-    give(0, row.me, row.sibling, mine)
+    give(0, row.me, mine)
     yield
     first()
     flight[1] = launch(row.partner, 0)
-    give(0, row.partner, row.across)
+    give(0, row.partner)
     yield
     for step in range(4):
-        for chain, base, other in ((0, row.me, row.sibling), (1, row.partner, row.across)):
+        for chain, base in ((0, row.me), (1, row.partner)):
             for landed in flight[chain]:
                 landed()
             if step < 3:
                 flight[chain] = launch(base, step + 1)
-                give(step + 1, row.along(base, -step - 1), row.along(other, -step - 1))
-                give(step + 1, row.along(base, step + 1), row.along(other, step + 1))
+                give(step + 1, row.along(base, -step - 1))
+                give(step + 1, row.along(base, step + 1))
             else:
-                give(4, row.along(base, 4), row.along(other, 4))
+                give(4, row.along(base, 4))
             yield
-
-
-def whole(origin):
-    return [(None, lambda ref: ref)]
-
-
-def rows_half(h):
-    return lambda origin: [(None, lambda ref: ref.at[pl.ds(16 * h, 16), :])]
 
 
 def split(x):
@@ -163,8 +173,8 @@
     return jnp.dot(a, b, preferred_element_type=jnp.float32)
 
 
-COPIES = 108
-ORDER = "PFWPFPFWFPWFWPFPWFWFRRRRFRRRRFUFFFUU"
+SENDS, RECVS = 36, 58
+ORDER = "PFWPFFPWFFWPWFPFWPFWRRRRRRRRFFUFFUU"
 BATCHES = ((0, -1, 1, -2, 2), (-3, 3, 4))
 SPAN = 1024
 
@@ -188,10 +198,7 @@
     for n in [row.sibling, row.partner] + [row.along(row.me, p) for p in planes]:
         pl.semaphore_signal(barrier, inc=1, device_id={"row": n}, device_id_type=MESH)
 
-    def to_cols(src_of, dst, peers=cols):
-        return [net.remote(src_of(c), dst, {"col": c}) for c in peers]
-
-    base = COPIES - PIVOTS
+    base = net.new_recv(PIVOTS)
 
     def owners_of(k):
         return piv[k] // blocks_dev
@@ -203,7 +210,7 @@
 
     def factor():
         keep = net.own(f, fo.at[row.me])
-        gather = row_gather(net, row, fo, whole, rows_half, f, given)
+        gather = row_gather(net, row, fo, f, given)
         next(gather)
         yield
         keep.wait()
@@ -244,20 +251,16 @@
                 sends.append((me == k, above, above, {"col": c}))
             net.some(sends, [], base + me)
         yield
-        hop = []
-        for k in range(1, PIVOTS):
-            above = pv.at[k, row.group, pl.ds(0, k)]
-            net.take([(me != k, above)], base + k)
-            hop.append(net.some([(None, above, above, {"row": row.partner})], [(None, above)]))
-        yield
-        last = []
-        for k, landed in zip(range(1, PIVOTS), hop):
-            landed()
-            above = pv.at[k, pl.ds(2 * row.core, 2), pl.ds(0, k)]
-            last.append(net.some([(None, above, above, {"row": row.sibling})], [(None, above)]))
-        yield
-        for landed in last:
-            landed()
+        above = [(k, pv.at[k, row.group, pl.ds(0, k)]) for k in range(1, PIVOTS)]
+        for k, ref in above:
+            net.take([(me != k, ref)], base + k)
+        across = net.group([(ref, ref, {"row": row.partner}) for _, ref in above], pv.at[0, :, pl.ds(0, PIVOTS - 1)])
+        yield
+        across.wait_recv()
+        above = [pv.at[k, pl.ds(2 * row.core, 2), pl.ds(0, k)] for k in range(1, PIVOTS)]
+        last = net.group([(ref, ref, {"row": row.sibling}) for ref in above], pv.at[0:2, :, pl.ds(0, PIVOTS - 1)])
+        yield
+        last.wait_recv()
         yield
 
     owners = [piv[k] // blocks_dev for k in range(PIVOTS)]
@@ -281,10 +284,14 @@
 
     def panels():
         load_w.wait()
-        hop = []
+        outs, lands = [net.new_send() for _ in range(2)], [net.new_recv() for _ in range(2)]
+        pairs = (q, rq), (s, rs)
         for c in cols:
             encode(c, q.at[c], s.at[c])
-            hop += to_cols(lambda c: s.at[c], rs.at[me], [c]) + to_cols(lambda c: q.at[c], rq.at[me], [c])
+            for out_sem, land, (here, there) in zip(outs, lands, pairs):
+                net.some([(None, here.at[c], there.at[me], {"col": c})], [], land, out_sem)
+        hop = [net.here(o, n, here.at[pl.ds(0, COLDEV - 1)]) for o, n, (here, _) in zip(outs, lands, pairs)]
+        net.sent += [once(copy) for copy in hop]
         encode(me, rq.at[me], rs.at[me])
         yield
         for copy in hop:
@@ -300,7 +307,7 @@
         beside_ahead, beside_behind = lax.rem(beside + 2, COLDEV), lax.rem(beside + 6, COLDEV)
         across = net.remote(selq, qv.at[me], {"col": beside})
         first = [net.remote(selq, qv.at[me], {"col": c}) for c in (ahead, behind)]
-        scales = to_cols(lambda c: sels, sv.at[me])
+        scales = [net.group([(sels, sv.at[me], {"col": c}) for c in cols], sv.at[pl.ds(0, COLDEV - 1)])]
         keep = [net.own(selq, qv.at[me]), net.own(sels, sv.at[me])]
         yield
         across.wait_recv()
@@ -387,17 +394,17 @@
                     wv[i * per + b] = block * by_tile(kept)
                 else:
                     wv[i * per + b] = block
+            if last:
+                for b in range(per):
+                    columns = pl.ds(pl.multiple_of((i * per + b) * BLOCK, BLOCK), BLOCK)
+                    pltpu.make_async_copy(wv.at[i * per + b], out.at[:, columns], local.at[15]).start()
 
     def update():
         for n, distances in enumerate(BATCHES):
             for d in sorted({abs(p) for p in distances}):
-                for landed in given[d]:
-                    landed()
+                given[d]()
             add(distances, n == len(BATCHES) - 1)
             yield
-        stores = []
-        for b in range(blocks_dev):
-            pltpu.make_async_copy(wv.at[b], out.at[:, pl.ds(b * BLOCK, BLOCK)], local.at[15]).start()
         pltpu.make_async_copy(wv, wv, local.at[15]).wait()
         yield
 
@@ -408,6 +415,7 @@
     for stream in streams.values():
         for _ in stream:
             pass
+    assert (net.sends, net.recvs) == (SENDS, RECVS), (net.sends, net.recvs)
     net.finish()
 
 
@@ -442,8 +450,8 @@
             s,
             pltpu.VMEM((PIVOTS, rows, 2 * BLOCK), jnp.bfloat16),
             pltpu.VMEM((ROWDEV, frows, width), f.dtype),
-            pltpu.SemaphoreType.DMA((COPIES,)),
-            pltpu.SemaphoreType.DMA((COPIES,)),
+            pltpu.SemaphoreType.DMA((SENDS,)),
+            pltpu.SemaphoreType.DMA((RECVS,)),
             pltpu.SemaphoreType.DMA((16,)),
         ],
         compiler_params=pltpu.CompilerParams(collective_id=0 if slots < PIVOTS else 1, has_side_effects=True, vmem_limit_bytes=VMEM),
@@ -455,8 +463,8 @@
 
 
 def shards(weights, factor_rows, diag_inverse, prune_tiles, pivot_order):
-    owners = pivot_order // (weights.shape[1] // BLOCK)
-    pairs = jnp.sum((owners[:, None] == owners[None, :]).astype(jnp.int32))
+    blocks_dev = weights.shape[1] // BLOCK
+    pairs = jnp.sum(((pivot_order[:, None] ^ pivot_order[None, :]) < blocks_dev).astype(jnp.int32))
     return lax.cond(
         pairs < (SLOTS + 1) ** 2 + PIVOTS - SLOTS - 1,
         functools.partial(comm, SLOTS),

time: 54.8 us -> 54.3 us (level); the launches traced: 54.1 us -> 54.2 us
    reduce_sum x1, other arithmetic: 0.7 us -> 1.43 us  [shards(): jnp.sum((pivot_order[:, None] ^ pivot_order[None, :] < blocks_dev).astype...]
    select_n x1 -> x0, other arithmetic: 0.66 us -> none  [shards(): owners = pivot_order // (weights.shape[1] // BLOCK)]
where the time goes in v4:
time: 54.3 us; the launch traced here: 54.2 us
  Pallas kernels  49.8 us (92%)
  local copies, waits for them, and re-layouts  2.02 us (4%)
  other arithmetic  1.43 us (3%)
  between operations  0.66 us (1%)
    pallas_call x1, Pallas kernels, comm(): pl.pallas_call(functools.partial(comm_kernel, slots), in_specs=[SM, SM, A...  49.8 us
    unnamed x1, local copies, waits for them, and re-layouts  2.02 us
    reduce_sum x1, other arithmetic, shards(): jnp.sum((pivot_order[:, None] ^ pivot_order[None, :] < blocks_dev).astype...  1.43 us

profile of v4, /device:TPU:2, one launch (start us, length us, event | category | flops | bytes accessed | tf_op | source)
XLA Modules:
  0.0 54.2 jit_solution(3561557903549768213)
XLA Ops:
  0.0 1.4 %convert_reduce_fusion = s32[]{:T(128)} fusion(s32[8]{0:T(128)} %param.11), kind=kLoop, calls=%fused_computation | loop fusion | flops 255 | bytes 36 | tf_op jit(solution)/shard_map/reduce_sum | solution.py:467
  2.1 50.1 %conditional.1 = (f32[512,2048]{1,0:T(8,128)S(1)}) conditional(s32[]{:T(128)} %convert_element_type.7, (s32[8]{0:T(128)}, s32[4,8]{1,0:T(4,128)}, f32[512,2048]{1,0:T(8,128)}, bf16[32,2048]{1,0:T(8,128)(2,1)}, bf16[8,128,128]{2,1,0:T(8,128)(2,1)}) %tuple.11, (s32[8]{0:T(128)}, s32[4,8]{1,0:T(4,128)}, f32[512,2048]{1,0:T(8,128)}, ...), branch_computations={%region_1.0_spmd, %region_2.0_spmd} | conditional | bytes 8 | solution.py:468
  2.1 49.8 %comm.3 = f32[512,2048]{1,0:T(8,128)S(1)} custom-call(s32[8]{0:T(128)} %get-tuple-element.33.piv, s32[4,8]{1,0:T(4,128)} %get-tuple-element.34.prune, f32[512,2048]{1,0:T(8,128)} %get-tuple-element.35.w, bf16[32,2048]{1,0:T(8,128)(2,1)} %get-tuple-element.36.f, bf16[8,128,128]{2,1,0:T(8,128)(2,1)} %get-tuple-element.37.d), custom_call_target="tpu_custom_call" | custom-call | tf_op jit(solution)/shard_map/cond/branch_1_fun/comm/pallas_call | solution.py:430
  52.2 2.0 %copy.11 = f32[512,2048]{1,0:T(8,128)} copy(f32[512,2048]{1,0:T(8,128)S(1)} %get-tuple-element.38) | data formatting | bytes 8388608

commit v5 on v4

--- a/solution.py
+++ b/solution.py
@@ -174,7 +174,7 @@
 
 
 SENDS, RECVS = 36, 58
-ORDER = "PFWPFFPWFFWPWFPFWPFWRRRRRRRRFFUFFUU"
+ORDER = "PFWPFFPWFFWFPWFPWFPWRRRRRRRRFFUFUU"
 BATCHES = ((0, -1, 1, -2, 2), (-3, 3, 4))
 SPAN = 1024
 

time: 54.3 us -> 54.2 us (level)
  no operation moved by 1% of the time
where the time goes in v5:
time: 54.2 us; the launch traced here: 54.1 us
  Pallas kernels  49.7 us (92%)
  local copies, waits for them, and re-layouts  2.02 us (4%)
  other arithmetic  1.43 us (3%)
  between operations  0.66 us (1%)
    pallas_call x1, Pallas kernels, comm(): pl.pallas_call(functools.partial(comm_kernel, slots), in_specs=[SM, SM, A...  49.7 us
    unnamed x1, local copies, waits for them, and re-layouts  2.02 us
    reduce_sum x1, other arithmetic, shards(): jnp.sum((pivot_order[:, None] ^ pivot_order[None, :] < blocks_dev).astype...  1.43 us

profile of v5, /device:TPU:2, one launch (start us, length us, event | category | flops | bytes accessed | tf_op | source)
XLA Modules:
  0.0 54.1 jit_solution(15410648493969131327)
XLA Ops:
  0.0 1.4 %convert_reduce_fusion = s32[]{:T(128)} fusion(s32[8]{0:T(128)} %param.11), kind=kLoop, calls=%fused_computation | loop fusion | flops 255 | bytes 36 | tf_op jit(solution)/shard_map/reduce_sum | solution.py:467
  2.1 50.0 %conditional.1 = (f32[512,2048]{1,0:T(8,128)S(1)}) conditional(s32[]{:T(128)} %convert_element_type.7, (s32[8]{0:T(128)}, s32[4,8]{1,0:T(4,128)}, f32[512,2048]{1,0:T(8,128)}, bf16[32,2048]{1,0:T(8,128)(2,1)}, bf16[8,128,128]{2,1,0:T(8,128)(2,1)}) %tuple.11, (s32[8]{0:T(128)}, s32[4,8]{1,0:T(4,128)}, f32[512,2048]{1,0:T(8,128)}, ...), branch_computations={%region_1.0_spmd, %region_2.0_spmd} | conditional | bytes 8 | solution.py:468
  2.1 49.7 %comm.3 = f32[512,2048]{1,0:T(8,128)S(1)} custom-call(s32[8]{0:T(128)} %get-tuple-element.33.piv, s32[4,8]{1,0:T(4,128)} %get-tuple-element.34.prune, f32[512,2048]{1,0:T(8,128)} %get-tuple-element.35.w, bf16[32,2048]{1,0:T(8,128)(2,1)} %get-tuple-element.36.f, bf16[8,128,128]{2,1,0:T(8,128)(2,1)} %get-tuple-element.37.d), custom_call_target="tpu_custom_call" | custom-call | tf_op jit(solution)/shard_map/cond/branch_1_fun/comm/pallas_call | solution.py:430
  52.1 2.0 %copy.11 = f32[512,2048]{1,0:T(8,128)} copy(f32[512,2048]{1,0:T(8,128)S(1)} %get-tuple-element.38) | data formatting | bytes 8388608
